TPU v7x, 128 devices: a whole 4x4x4 slice. The times are simulated.
128 devices in a mesh: pb: 16 (over z_hi, y, core), ka: 8 (over z_lo, x).
Axes of the slice: x: 4, y: 4, z: 4 (z_hi: 2, z_lo: 2; z = z_hi * 2 + z_lo), core: 2. Of those that a mesh axis runs over, the one named last changes fastest.
Arguments:
- query_features: bfloat16 [128, 192, 256], P('pb'), may hold values from -6 to 6
- key_features: bfloat16 [192, 128, 256], P(None, 'ka'), may hold values from -6 to 6
- pyramid_grad: bfloat16 [24576, 8, 4080], P('pb', 'ka'), may hold values from -13.0639453 to 13.0639453
- query_image: bfloat16 [128, 192, 256], P('pb', 'ka'), may hold values from -0.0625 to 0.0625
- key_image: bfloat16 [192, 128, 256], P('pb', 'ka'), may hold values from -0.0625 to 0.0625
- conv_weight: bfloat16 [3, 3, 256, 256], replicated, may hold values from -0.125 to 0.125
Outputs:
- query_image_grad: bfloat16 [128, 192, 256], P('pb', 'ka')
- key_image_grad: bfloat16 [192, 128, 256], P('pb', 'ka')
- weight_grad: float32 [3, 3, 256, 256], replicated
All inputs are finite; a program needn't handle non-finite values.
Results may differ from a plain program's by a relative error of at most 0.0056.
Values may be sent and summed in bfloat16 or wider, within the bound.
A program may use at most 128 MiB of HBM per device.

v0:
```python
import jax
import jax.numpy as jnp
from jax import lax
from jax.sharding import PartitionSpec as P

D = 256
LEVELS = 4


def padded(cells, sides, width):
    for axis, dim in sides:
        count = lax.axis_size(axis)
        ends = count - 1
        head = lax.slice_in_dim(cells, 0, width, axis=dim)
        tail = lax.slice_in_dim(cells, cells.shape[dim] - width, cells.shape[dim], axis=dim)
        cells = jnp.concatenate(
            [
                lax.ppermute(tail, axis, [(i, (i + 1) % count) for i in range(ends)]),
                cells,
                lax.ppermute(head, axis, [((i + 1) % count, i) for i in range(ends)]),
            ],
            axis=dim,
        )
    return cells


def pool_levels(strip):
    strip_float = strip.astype(jnp.float32)
    result = []
    for level_index in range(LEVELS):
        factor = 2**level_index
        cell_cols, key_rows, channels = strip_float.shape
        pooled = strip_float.reshape(
            cell_cols // factor, factor, key_rows // factor, factor, channels
        ).mean(axis=(1, 3))
        result.append(pooled.astype(jnp.bfloat16))
    return result


def conv_backward(padded_input, padded_grad, kernel):
    tile_rows = padded_grad.shape[0] - 2
    tile_cols = padded_grad.shape[1] - 2
    out_channels = padded_grad.shape[2]
    in_channels = kernel.shape[2]
    interior = padded_grad[1 : 1 + tile_rows, 1 : 1 + tile_cols].reshape(-1, out_channels)
    input_acc = jnp.zeros((tile_rows * tile_cols, in_channels), jnp.float32)
    kernel_rows = []
    for row_shift in range(3):
        kernel_row = []
        for col_shift in range(3):
            shifted = padded_grad[
                2 - row_shift : 2 - row_shift + tile_rows, 2 - col_shift : 2 - col_shift + tile_cols
            ].reshape(-1, out_channels)
            input_acc = input_acc + lax.dot_general(
                shifted,
                kernel[row_shift, col_shift],
                (((1,), (1,)), ((), ())),
                preferred_element_type=jnp.float32,
            )
            window = padded_input[
                row_shift : row_shift + tile_rows, col_shift : col_shift + tile_cols
            ].reshape(-1, in_channels)
            weight_term = lax.dot_general(
                window, interior, (((0,), (0,)), ((), ())), preferred_element_type=jnp.float32
            )
            kernel_row.append(weight_term)
        kernel_rows.append(jnp.stack(kernel_row))
    return (input_acc.reshape(tile_rows, tile_cols, in_channels), jnp.stack(kernel_rows))


def body(query_features, key_features, pyramid_grad, query_image, key_image, conv_weight):
    norm_scale = D ** (-0.5)
    strip_rows, width_cells, channels = query_features.shape
    key_rows = key_features.shape[1]
    queries = query_features.reshape(strip_rows * width_cells, channels)
    strip_grads = pyramid_grad.reshape(pyramid_grad.shape[0], pyramid_grad.shape[2])
    pooled = pool_levels(key_features)
    query_part = jnp.zeros((queries.shape[0], channels), jnp.float32)
    coarse_sum = jnp.zeros((width_cells, key_rows, channels), jnp.float32)
    level_zero = None
    offset = 0
    for level_index in range(LEVELS):
        factor = 2**level_index
        grid_rows = key_rows // factor
        grid_cols = width_cells // factor
        cell_count = grid_rows * grid_cols
        grad_block = strip_grads[:, offset : offset + cell_count]
        offset = offset + cell_count
        ordered = jnp.transpose(pooled[level_index], (1, 0, 2)).reshape(cell_count, channels)
        query_part = query_part + jnp.dot(grad_block, ordered, preferred_element_type=jnp.float32)
        if level_index == 0:
            level_zero = grad_block.reshape(-1, grid_rows, grid_cols)
        else:
            coarse = lax.dot_general(
                grad_block, queries, (((0,), (0,)), ((), ())), preferred_element_type=jnp.float32
            )
            coarse = jnp.transpose(coarse.reshape(grid_rows, grid_cols, channels), (1, 0, 2))
            spread = jnp.broadcast_to(
                coarse[:, None, :, None, :], (grid_cols, factor, grid_rows, factor, channels)
            ).reshape(width_cells, key_rows, channels)
            coarse_sum = coarse_sum + spread / 4.0**level_index
    query_grad = lax.psum_scatter(
        (query_part * norm_scale).reshape(strip_rows, width_cells, channels),
        "ka",
        scatter_dimension=1,
        tiled=True,
    ).astype(jnp.bfloat16)
    fine_term = jnp.einsum("qhw,qd->whd", level_zero, queries, preferred_element_type=jnp.float32)
    key_grad = lax.psum_scatter(
        (fine_term + coarse_sum) * norm_scale, "pb", scatter_dimension=0, tiled=True
    ).astype(jnp.bfloat16)
    padded_query_image, padded_query_grad, padded_key_image, padded_key_grad = (
        padded(query_image, (("pb", 0), ("ka", 1)), 1),
        padded(query_grad, (("pb", 0), ("ka", 1)), 1),
        padded(key_image, (("pb", 0), ("ka", 1)), 1),
        padded(key_grad, (("pb", 0), ("ka", 1)), 1),
    )
    kernel_swapped = jnp.transpose(conv_weight, (1, 0, 2, 3))
    grad_first, weight_first = conv_backward(padded_query_image, padded_query_grad, conv_weight)
    grad_second, weight_swapped = conv_backward(padded_key_image, padded_key_grad, kernel_swapped)
    local_weight = weight_first + jnp.transpose(weight_swapped, (1, 0, 2, 3))
    weight_grad = lax.psum(local_weight, ("pb", "ka"))
    return (grad_first.astype(jnp.bfloat16), grad_second.astype(jnp.bfloat16), weight_grad)


def solution(mesh):
    placed = (
        P("pb", None, None),
        P(None, "ka", None),
        P("pb", "ka", None),
        P("pb", "ka", None),
        P("pb", "ka", None),
        P(),
    )
    return jax.shard_map(
        body,
        mesh=mesh,
        in_specs=placed,
        out_specs=(P("pb", "ka", None), P("pb", "ka", None), P()),
        check_vma=False,
    )
```

profile of v0, /device:TPU:1, one launch (start us, length us, event | category | flops | bytes accessed | tf_op | source)
XLA Modules:
  0.0 347.2 jit_solution(3468012486653483771)
XLA Ops:
  7.2 4.6 %reshape.140 = f32[96,2,8,2,256]{4,3,2,1,0:T(2,128)} reshape(bf16[192,16,256]{2,1,0:T(8,128)(2,1)} %param.7) | data formatting | bytes 4718592 | tf_op jit(solution)/shard_map/reshape | solution.py:33
  13.5 2.5 reshape.142
  16.0 2.2 convert_element_type.43
  18.2 4.4 %reduce_sum.27 = f32[96,8,256]{2,1,0:T(8,128)S(1)} reduce(f32[96,2,8,2,256]{4,3,2,1,0:T(2,128)} %reshape.140, f32[]{:T(128)} %constant.6.clone.1), dimensions={1,3}, to_apply=%region_0.0 | reduce | flops 589824 | bytes 3932164 | tf_op jit(solution)/shard_map/reduce_sum | solution.py:35
  22.7 3.0 reduce_sum.32
  25.8 2.4 reduce_sum.33
  28.2 2.8 convolution_bitcast_fusion.2
  31.1 5.2 %fusion.4 = f32[1536,256]{1,0:T(8,128)S(1)} fusion(f32[1536,256]{1,0:T(8,128)S(1)} %convolution_bitcast_fusion.2, bf16[3072,256]{1,0:T(8,128)(2,1)S(1)} %bitcast.277, bf16[1536,4080]{0,1:T(8,128)(2,1)} %bitcast.279), kind=kOutput, calls=%fused_computation.5 | convolution fusion | flops 2416312320 | bytes 14155776 | tf_op jit(solution)/shard_map/dot_general | solution.py:90
  37.8 2.5 fusion.8
  41.2 4.6 %collective-permute-start.12 = (bf16[1,16,256]{2,1,0:T(8,128)(2,1)S(1)}, bf16[1,16,256]{2,1,0:T(8,128)(2,1)S(1)}, u32[]{:S(2)}, u32[]{:S(2)}) collective-permute-start(bf16[1,16,256]{2,1,0:T(8,128)(2,1)S(1)} %get-tuple-element.28), channel_id=1, source_target_pairs={{0,8},{8,16},{16,24},{24,32},{32,40},{40,48},{48,56},{56,64},{64,7... | collective-permute-start | bytes 24584 | tf_op jit(solution)/shard_map/ppermute | solution.py:18
  45.8 1.9 collective-permute-start.13
  47.7 3.6 %collective-permute-start.8 = (bf16[1,24,256]{2,1,0:T(8,128)(2,1)S(1)}, bf16[1,24,256]{2,1,0:T(8,128)(2,1)S(1)}, u32[]{:S(2)}, u32[]{:S(2)}) collective-permute-start(bf16[1,24,256]{2,1,0:T(8,128)(2,1)S(1)} %get-tuple-element.30), channel_id=1, source_target_pairs={{0,8},{8,16},{16,24},{24,32},{32,40},{40,48},{48,56},{56,64},{64,7... | collective-permute-start | bytes 36872 | tf_op jit(solution)/shard_map/ppermute | solution.py:18
  51.4 2.1 collective-permute-start.9
  53.5 1.8 slice.313
  58.1 2.9 broadcast_in_dim.6
  61.1 5.3 %div.61 = f32[192,16,256]{2,0,1:T(8,128)} reshape(f32[96,2,8,2,256]{4,1,0,3,2:T(2,128)} %broadcast_in_dim.6) | data formatting | bytes 6291456 | tf_op jit(solution)/shard_map/div | solution.py:101
  66.7 2.3 broadcast_in_dim.7
  69.0 5.0 %div.65 = f32[192,16,256]{2,0,1:T(8,128)} reshape(f32[48,4,4,4,256]{4,1,0,3,2:T(4,128)} %broadcast_in_dim.7) | data formatting | bytes 6291456 | tf_op jit(solution)/shard_map/div | solution.py:101
  74.2 5.4 %fusion = f32[256,3072]{0,1:S(1)} fusion(bf16[1536,256]{1,0:T(8,128)(2,1)S(1)} %bitcast.256, bf16[1536,4080]{0,1:T(8,128)(2,1)} %bitcast.285), kind=kOutput, calls=%fused_computation | convolution fusion | flops 2415919104 | bytes 13369344
  82.4 3.5 copy.54
  86.1 3.7 %collective-permute-start.14 = (bf16[14,1,256]{2,1,0:T(2,128)(2,1)S(1)}, bf16[14,1,256]{2,1,0:T(2,128)(2,1)}, u32[]{:S(2)}, u32[]{:S(2)}) collective-permute-start(bf16[14,1,256]{2,1,0:T(2,128)(2,1)S(1)} %get-tuple-element.21), channel_id=1, source_target_pairs={{0,1},{1,2},{2,3},{3,4},{4,5},{5,6},{6,7},{8,9},{9,10},{10,11},{11... | collective-permute-start | bytes 21512 | tf_op jit(solution)/shard_map/ppermute | solution.py:18
  92.5 4.6 %collective-permute-start.10 = (bf16[10,1,256]{2,1,0:T(2,128)(2,1)S(1)}, bf16[10,1,256]{2,1,0:T(2,128)(2,1)S(1)}, u32[]{:S(2)}, u32[]{:S(2)}) collective-permute-start(bf16[10,1,256]{2,1,0:T(2,128)(2,1)S(1)} %get-tuple-element.15), channel_id=1, source_target_pairs={{0,1},{1,2},{2,3},{3,4},{4,5},{5,6},{6,7},{8,9},{9,10},{10,11},{11... | collective-permute-start | bytes 15368 | tf_op jit(solution)/shard_map/ppermute | solution.py:18
  98.1 4.5 %collective-permute-start = (bf16[1,24,256]{2,1,0:T(8,128)(2,1)S(1)}, bf16[1,24,256]{2,1,0:T(8,128)(2,1)S(1)}, u32[]{:S(2)}, u32[]{:S(2)}) collective-permute-start(bf16[1,24,256]{2,1,0:T(8,128)(2,1)S(1)} %get-tuple-element.37), channel_id=1, source_target_pairs={{0,8},{8,16},{16,24},{24,32},{32,40},{40,48},{48,56},{56,64},{64,7... | collective-permute-start | bytes 36872 | tf_op jit(solution)/shard_map/ppermute | solution.py:18
  102.6 1.9 collective-permute-start.1
  109.3 4.3 %collective-permute-start.3 = (bf16[10,1,256]{2,1,0:T(2,128)(2,1)S(1)}, bf16[10,1,256]{2,1,0:T(2,128)(2,1)S(1)}, u32[]{:S(2)}, u32[]{:S(2)}) collective-permute-start(bf16[10,1,256]{2,1,0:T(2,128)(2,1)S(1)} %get-tuple-element.20), channel_id=1, source_target_pairs={{0,1},{1,2},{2,3},{3,4},{4,5},{5,6},{6,7},{8,9},{9,10},{10,11},{11... | collective-permute-start | bytes 15368 | tf_op jit(solution)/shard_map/ppermute | solution.py:18
  116.9 49.9 %reduce-scatter.5.cloned.1.call-done = f32[12,16,256]{2,1,0:T(8,128)} async-done(((f32[192,16,256]{2,1,0:T(8,128)}), f32[12,16,256]{2,1,0:T(8,128)}) %reduce-scatter.5.cloned.1.call-update) | async-done | bytes 196624 | tf_op jit(solution)/shard_map/reduce_scatter | solution.py:109
  168.0 4.9 %collective-permute-start.4 = (bf16[1,16,256]{2,1,0:T(8,128)(2,1)S(1)}, bf16[1,16,256]{2,1,0:T(8,128)(2,1)S(1)}, u32[]{:S(2)}, u32[]{:S(2)}) collective-permute-start(bf16[1,16,256]{2,1,0:T(8,128)(2,1)S(1)} %get-tuple-element.33), channel_id=1, source_target_pairs={{0,8},{8,16},{16,24},{24,32},{32,40},{40,48},{48,56},{56,64},{64,7... | collective-permute-start | bytes 24584 | tf_op jit(solution)/shard_map/ppermute | solution.py:18
  172.9 1.9 collective-permute-start.5
  182.2 1.7 maximum_add_fusion
  185.3 4.0 %collective-permute-start.7 = (bf16[14,1,256]{2,1,0:T(2,128)(2,1)S(1)}, bf16[14,1,256]{2,1,0:T(2,128)(2,1)S(1)}, u32[]{:S(2)}, u32[]{:S(2)}) collective-permute-start(bf16[14,1,256]{2,1,0:T(2,128)(2,1)S(1)} %get-tuple-element.26), channel_id=1, source_target_pairs={{0,1},{1,2},{2,3},{3,4},{4,5},{5,6},{6,7},{8,9},{9,10},{10,11},{11... | collective-permute-start | bytes 21512 | tf_op jit(solution)/shard_map/ppermute | solution.py:18
  192.6 144.7 %all-reduce.2.cloned.1.call-done = f32[3,3,256,256]{3,2,1,0:T(8,128)} async-done(((f32[3,3,256,256]{3,2,1,0:T(8,128)}), f32[3,3,256,256]{3,2,1,0:T(8,128)}) %all-reduce.2.cloned.1.call-update) | async-done | bytes 2359312 | tf_op jit(solution)/shard_map/psum | solution.py:122
  337.4 3.3 copy.73
  (130 shorter events, 35.2 us)
Async XLA Ops:
  7.2 50.2 %copy-start = (bf16[8,192,256]{2,1,0:T(8,128)(2,1)S(1)}, bf16[8,192,256]{2,1,0:T(8,128)(2,1)}, u32[]{:S(2)}) copy-start(bf16[8,192,256]{2,1,0:T(8,128)(2,1)} %param.6) | copy-start | bytes 2359300
  7.2 4.7 %copy-start.2 = (bf16[192,16,256]{2,1,0:T(8,128)(2,1)S(1)}, bf16[192,16,256]{2,1,0:T(8,128)(2,1)}, u32[]{:S(2)}) copy-start(bf16[192,16,256]{2,1,0:T(8,128)(2,1)} %param.7) | copy-start | bytes 4718596
  7.2 90.0 %reduce-scatter.3.cloned.1.call-start = ((), (), s32[]{:S(2)}) async-start(), calls=%async_computation.2 | async-start | bytes 1769472 | tf_op jit(solution)/shard_map/reduce_scatter | solution.py:102
  28.2 2.8 copy-start.7
  40.3 0.9 copy-start.9
  40.3 7.4 %copy-start.8 = (bf16[8,24,256]{2,1,0:T(8,128)(2,1)S(1)}, bf16[8,24,256]{2,1,0:T(8,128)(2,1)}, u32[]{:S(2)}) copy-start(bf16[8,24,256]{2,1,0:T(8,128)(2,1)} %param.9) | copy-start | bytes 294916
  40.3 126.4 %reduce-scatter.5.cloned.1.call-start = ((), (), s32[]{:S(2)}) async-start(), calls=%async_computation.3 | async-start | bytes 3342336 | tf_op jit(solution)/shard_map/reduce_scatter | solution.py:109
  41.2 44.8 %collective-permute-start.12 = (bf16[1,16,256]{2,1,0:T(8,128)(2,1)S(1)}, bf16[1,16,256]{2,1,0:T(8,128)(2,1)S(1)}, u32[]{:S(2)}, u32[]{:S(2)}) collective-permute-start(bf16[1,16,256]{2,1,0:T(8,128)(2,1)S(1)} %get-tuple-element.28), channel_id=1, source_target_pairs={{0,8},{8,16},{16,24},{24,32},{32,40},{40,48},{48,56},{56,64},{64,7... | collective-permute-start | bytes 24584 | tf_op jit(solution)/shard_map/ppermute | solution.py:18
  45.8 40.2 %collective-permute-start.13 = (bf16[1,16,256]{2,1,0:T(8,128)(2,1)S(1)}, bf16[1,16,256]{2,1,0:T(8,128)(2,1)S(1)}, u32[]{:S(2)}, u32[]{:S(2)}) collective-permute-start(bf16[1,16,256]{2,1,0:T(8,128)(2,1)S(1)} %get-tuple-element.27), channel_id=1, source_target_pairs={{8,0},{16,8},{24,16},{32,24},{40,32},{48,40},{56,48},{64,56},{72,6... | collective-permute-start | bytes 24584 | tf_op jit(solution)/shard_map/ppermute | solution.py:20
  47.7 43.4 %collective-permute-start.8 = (bf16[1,24,256]{2,1,0:T(8,128)(2,1)S(1)}, bf16[1,24,256]{2,1,0:T(8,128)(2,1)S(1)}, u32[]{:S(2)}, u32[]{:S(2)}) collective-permute-start(bf16[1,24,256]{2,1,0:T(8,128)(2,1)S(1)} %get-tuple-element.30), channel_id=1, source_target_pairs={{0,8},{8,16},{16,24},{24,32},{32,40},{40,48},{48,56},{56,64},{64,7... | collective-permute-start | bytes 36872 | tf_op jit(solution)/shard_map/ppermute | solution.py:18
  51.4 39.8 %collective-permute-start.9 = (bf16[1,24,256]{2,1,0:T(8,128)(2,1)S(1)}, bf16[1,24,256]{2,1,0:T(8,128)(2,1)S(1)}, u32[]{:S(2)}, u32[]{:S(2)}) collective-permute-start(bf16[1,24,256]{2,1,0:T(8,128)(2,1)S(1)} %get-tuple-element.29), channel_id=1, source_target_pairs={{8,0},{16,8},{24,16},{32,24},{40,32},{48,40},{56,48},{64,56},{72,6... | collective-permute-start | bytes 36872 | tf_op jit(solution)/shard_map/ppermute | solution.py:20
  74.2 5.7 %copy-start.4 = (f32[192,16,256]{2,0,1:T(8,128)S(1)}, f32[192,16,256]{2,0,1:T(8,128)}, u32[]{:S(2)}) copy-start(f32[192,16,256]{2,0,1:T(8,128)} %div.65) | copy-start | bytes 9437188
  79.6 1.9 copy-start.3
  85.9 251.4 %all-reduce.2.cloned.1.call-start = ((), (), s32[]{:S(2)}) async-start(), calls=%async_computation.4 | async-start | bytes 4718592 | tf_op jit(solution)/shard_map/psum | solution.py:122
  86.0 19.2 %copy-start.11 = (bf16[14,16,256]{2,1,0:T(8,128)(2,1)}, bf16[14,16,256]{2,1,0:T(8,128)(2,1)S(1)}, u32[]{:S(2)}) copy-start(bf16[14,16,256]{2,1,0:T(8,128)(2,1)S(1)} %constant_dynamic-update-slice_fusion.3) | copy-start | bytes 344068
  86.1 89.9 %collective-permute-start.14 = (bf16[14,1,256]{2,1,0:T(2,128)(2,1)S(1)}, bf16[14,1,256]{2,1,0:T(2,128)(2,1)}, u32[]{:S(2)}, u32[]{:S(2)}) collective-permute-start(bf16[14,1,256]{2,1,0:T(2,128)(2,1)S(1)} %get-tuple-element.21), channel_id=1, source_target_pairs={{0,1},{1,2},{2,3},{3,4},{4,5},{5,6},{6,7},{8,9},{9,10},{10,11},{11... | collective-permute-start | bytes 21512 | tf_op jit(solution)/shard_map/ppermute | solution.py:18
  89.8 85.2 %collective-permute-start.15 = (bf16[14,1,256]{2,1,0:T(2,128)(2,1)S(1)}, bf16[14,1,256]{2,1,0:T(2,128)(2,1)}, u32[]{:S(2)}, u32[]{:S(2)}) collective-permute-start(bf16[14,1,256]{2,1,0:T(2,128)(2,1)S(1)} %get-tuple-element.22), channel_id=1, source_target_pairs={{1,0},{2,1},{3,2},{4,3},{5,4},{6,5},{7,6},{9,8},{10,9},{11,10},{12... | collective-permute-start | bytes 21512 | tf_op jit(solution)/shard_map/ppermute | solution.py:20
  91.2 11.4 %collective-permute-start.11 = (bf16[10,1,256]{2,1,0:T(2,128)(2,1)S(1)}, bf16[10,1,256]{2,1,0:T(2,128)(2,1)S(1)}, u32[]{:S(2)}, u32[]{:S(2)}) collective-permute-start(bf16[10,1,256]{2,1,0:T(2,128)(2,1)S(1)} %get-tuple-element.16), channel_id=1, source_target_pairs={{1,0},{2,1},{3,2},{4,3},{5,4},{6,5},{7,6},{9,8},{10,9},{11,10},{12... | collective-permute-start | bytes 15368 | tf_op jit(solution)/shard_map/ppermute | solution.py:20
  92.5 12.5 %collective-permute-start.10 = (bf16[10,1,256]{2,1,0:T(2,128)(2,1)S(1)}, bf16[10,1,256]{2,1,0:T(2,128)(2,1)S(1)}, u32[]{:S(2)}, u32[]{:S(2)}) collective-permute-start(bf16[10,1,256]{2,1,0:T(2,128)(2,1)S(1)} %get-tuple-element.15), channel_id=1, source_target_pairs={{0,1},{1,2},{2,3},{3,4},{4,5},{5,6},{6,7},{8,9},{9,10},{10,11},{11... | collective-permute-start | bytes 15368 | tf_op jit(solution)/shard_map/ppermute | solution.py:18
  98.1 9.7 %collective-permute-start = (bf16[1,24,256]{2,1,0:T(8,128)(2,1)S(1)}, bf16[1,24,256]{2,1,0:T(8,128)(2,1)S(1)}, u32[]{:S(2)}, u32[]{:S(2)}) collective-permute-start(bf16[1,24,256]{2,1,0:T(8,128)(2,1)S(1)} %get-tuple-element.37), channel_id=1, source_target_pairs={{0,8},{8,16},{16,24},{24,32},{32,40},{40,48},{48,56},{56,64},{64,7... | collective-permute-start | bytes 36872 | tf_op jit(solution)/shard_map/ppermute | solution.py:18
  102.6 5.2 %collective-permute-start.1 = (bf16[1,24,256]{2,1,0:T(8,128)(2,1)S(1)}, bf16[1,24,256]{2,1,0:T(8,128)(2,1)S(1)}, u32[]{:S(2)}, u32[]{:S(2)}) collective-permute-start(bf16[1,24,256]{2,1,0:T(8,128)(2,1)S(1)} %get-tuple-element.38), channel_id=1, source_target_pairs={{8,0},{16,8},{24,16},{32,24},{40,32},{48,40},{56,48},{64,56},{72,6... | collective-permute-start | bytes 36872 | tf_op jit(solution)/shard_map/ppermute | solution.py:20
  107.5 6.1 %copy-start.5 = (bf16[3,3,256,256]{3,2,1,0:T(8,128)(2,1)S(1)}, bf16[3,3,256,256]{3,2,1,0:T(8,128)(2,1)}, u32[]{:S(2)}) copy-start(bf16[3,3,256,256]{3,2,1,0:T(8,128)(2,1)} %param.11) | copy-start | bytes 3538948
  107.9 6.0 %collective-permute-start.2 = (bf16[10,1,256]{2,1,0:T(2,128)(2,1)S(1)}, bf16[10,1,256]{2,1,0:T(2,128)(2,1)S(1)}, u32[]{:S(2)}, u32[]{:S(2)}) collective-permute-start(bf16[10,1,256]{2,1,0:T(2,128)(2,1)S(1)} %get-tuple-element.19), channel_id=1, source_target_pairs={{1,0},{2,1},{3,2},{4,3},{5,4},{6,5},{7,6},{9,8},{10,9},{11,10},{12... | collective-permute-start | bytes 15368 | tf_op jit(solution)/shard_map/ppermute | solution.py:20
  109.3 5.1 %collective-permute-start.3 = (bf16[10,1,256]{2,1,0:T(2,128)(2,1)S(1)}, bf16[10,1,256]{2,1,0:T(2,128)(2,1)S(1)}, u32[]{:S(2)}, u32[]{:S(2)}) collective-permute-start(bf16[10,1,256]{2,1,0:T(2,128)(2,1)S(1)} %get-tuple-element.20), channel_id=1, source_target_pairs={{0,1},{1,2},{2,3},{3,4},{4,5},{5,6},{6,7},{8,9},{9,10},{10,11},{11... | collective-permute-start | bytes 15368 | tf_op jit(solution)/shard_map/ppermute | solution.py:18
  115.4 52.3 %copy-start.10 = (bf16[12,16,256]{2,1,0:T(8,128)(2,1)S(1)}, bf16[12,16,256]{2,1,0:T(8,128)(2,1)}, u32[]{:S(2)}) copy-start(bf16[12,16,256]{2,1,0:T(8,128)(2,1)} %param.10) | copy-start | bytes 294916
  116.0 59.0 %copy-start.12 = (bf16[14,16,256]{2,1,0:T(8,128)(2,1)S(1)}, bf16[14,16,256]{2,1,0:T(8,128)(2,1)}, u32[]{:S(2)}) copy-start(bf16[14,16,256]{2,1,0:T(8,128)(2,1)} %copy-done.11) | copy-start | bytes 344068
  168.0 16.0 %collective-permute-start.4 = (bf16[1,16,256]{2,1,0:T(8,128)(2,1)S(1)}, bf16[1,16,256]{2,1,0:T(8,128)(2,1)S(1)}, u32[]{:S(2)}, u32[]{:S(2)}) collective-permute-start(bf16[1,16,256]{2,1,0:T(8,128)(2,1)S(1)} %get-tuple-element.33), channel_id=1, source_target_pairs={{0,8},{8,16},{16,24},{24,32},{32,40},{40,48},{48,56},{56,64},{64,7... | collective-permute-start | bytes 24584 | tf_op jit(solution)/shard_map/ppermute | solution.py:18
  172.9 11.0 %collective-permute-start.5 = (bf16[1,16,256]{2,1,0:T(8,128)(2,1)S(1)}, bf16[1,16,256]{2,1,0:T(8,128)(2,1)S(1)}, u32[]{:S(2)}, u32[]{:S(2)}) collective-permute-start(bf16[1,16,256]{2,1,0:T(8,128)(2,1)S(1)} %get-tuple-element.34), channel_id=1, source_target_pairs={{8,0},{16,8},{24,16},{32,24},{40,32},{48,40},{56,48},{64,56},{72,6... | collective-permute-start | bytes 24584 | tf_op jit(solution)/shard_map/ppermute | solution.py:20
  181.0 1.1 copy-start.6
  184.0 5.5 %collective-permute-start.6 = (bf16[14,1,256]{2,1,0:T(2,128)(2,1)S(1)}, bf16[14,1,256]{2,1,0:T(2,128)(2,1)S(1)}, u32[]{:S(2)}, u32[]{:S(2)}) collective-permute-start(bf16[14,1,256]{2,1,0:T(2,128)(2,1)S(1)} %get-tuple-element.25), channel_id=1, source_target_pairs={{1,0},{2,1},{3,2},{4,3},{5,4},{6,5},{7,6},{9,8},{10,9},{11,10},{12... | collective-permute-start | bytes 21512 | tf_op jit(solution)/shard_map/ppermute | solution.py:20
  185.3 4.8 %collective-permute-start.7 = (bf16[14,1,256]{2,1,0:T(2,128)(2,1)S(1)}, bf16[14,1,256]{2,1,0:T(2,128)(2,1)S(1)}, u32[]{:S(2)}, u32[]{:S(2)}) collective-permute-start(bf16[14,1,256]{2,1,0:T(2,128)(2,1)S(1)} %get-tuple-element.26), channel_id=1, source_target_pairs={{0,1},{1,2},{2,3},{3,4},{4,5},{5,6},{6,7},{8,9},{9,10},{10,11},{11... | collective-permute-start | bytes 21512 | tf_op jit(solution)/shard_map/ppermute | solution.py:18
  337.4 3.3 copy-start.1
Sparse Core Ops, SparseCore 0:
  40.5 39.0 reduce-scatter.2
  86.0 80.6 reduce-scatter.4
  184.0 153.2 all-reduce.1
where the time goes:
time: 349 us; the launch traced here: 347 us
  waiting for transfers between devices  196 us (56%)
  starting transfers between devices  47.5 us (14%)
  local copies, waits for them, and re-layouts  38.9 us (11%)
  matrix products  32.2 us (9%)
  other arithmetic  18.1 us (5%)
  between operations  14.6 us (4%)
    psum x1, waiting for transfers between devices, body(): weight_grad = lax.psum(local_weight, ('pb', 'ka'))  145 us
    reduce_scatter x1, waiting for transfers between devices, body(): lax.psum_scatter((fine_term + coarse_sum) * norm_scale, 'pb', scatter_dim...  49.9 us
    ppermute x8, starting transfers between devices, padded(): lax.ppermute(tail, axis, [(i, (i + 1) % count) for i in range(ends)])  34.2 us
    ppermute x8, starting transfers between devices, padded(): lax.ppermute(head, axis, [((i + 1) % count, i) for i in range(ends)])  13.2 us
    dot_general x4, matrix products, body(): jnp.dot(grad_block, ordered, preferred_element_type=jnp.float32)  12 us
    div x2, local copies, waits for them, and re-layouts, body(): coarse_sum = coarse_sum + spread / 4.0 ** level_index  10.2 us
    reduce_sum x3, other arithmetic, pool_levels(): pooled = strip_float.reshape(cell_cols // factor, factor, key_rows // fac...  9.77 us
    unnamed x32, local copies, waits for them, and re-layouts  8.44 us
  transfers between devices with their start and end apart: 19, of which 4 were waited for; matrix products, arithmetic and copies ran while one was open for 14% of the time, Pallas kernels for 0%

commit v1 on v0

--- a/solution.py
+++ b/solution.py
@@ -119,7 +119,7 @@
     grad_first, weight_first = conv_backward(padded_query_image, padded_query_grad, conv_weight)
     grad_second, weight_swapped = conv_backward(padded_key_image, padded_key_grad, kernel_swapped)
     local_weight = weight_first + jnp.transpose(weight_swapped, (1, 0, 2, 3))
-    weight_grad = lax.psum(local_weight, ("pb", "ka"))
+    weight_grad = lax.psum(lax.psum(local_weight, "ka"), "pb")
     return (grad_first.astype(jnp.bfloat16), grad_second.astype(jnp.bfloat16), weight_grad)
 
 

time: 349 us -> 414 us (1.19)
  waiting for transfers between devices: 196 us -> 258 us
    psum x1 -> x2, waiting for transfers between devices: 145 us -> 210 us  [body(): weight_grad = lax.psum(lax.psum(local_weight, 'ka'), 'pb')]
    reduce_scatter x1, waiting for transfers between devices: 49.9 us -> 44.7 us  [body(): lax.psum_scatter((fine_term + coarse_sum) * norm_scale, 'pb', scatter_dim...]
    unnamed x32 -> x54, local copies, waits for them, and re-layouts: 8.44 us -> 10.1 us
  transfers between devices with their start and end apart: 19 -> 20, of which waited for: 4 -> 4; matrix products, arithmetic and copies ran while one was open for 14% -> 11% of each run, Pallas kernels for 0% -> 0%
where the time goes in v1:
time: 414 us; the launch traced here: 413 us
  waiting for transfers between devices  258 us (62%)
  starting transfers between devices  47.5 us (11%)
  local copies, waits for them, and re-layouts  41.8 us (10%)
  matrix products  32.4 us (8%)
  other arithmetic  18.7 us (5%)
  between operations  14.8 us (4%)
    psum x2, waiting for transfers between devices, body(): weight_grad = lax.psum(lax.psum(local_weight, 'ka'), 'pb')  210 us
    reduce_scatter x1, waiting for transfers between devices, body(): lax.psum_scatter((fine_term + coarse_sum) * norm_scale, 'pb', scatter_dim...  44.7 us
    ppermute x8, starting transfers between devices, padded(): lax.ppermute(tail, axis, [(i, (i + 1) % count) for i in range(ends)])  34.2 us
    ppermute x8, starting transfers between devices, padded(): lax.ppermute(head, axis, [((i + 1) % count, i) for i in range(ends)])  13.2 us
    dot_general x4, matrix products, body(): jnp.dot(grad_block, ordered, preferred_element_type=jnp.float32)  12 us
    div x2, local copies, waits for them, and re-layouts, body(): coarse_sum = coarse_sum + spread / 4.0 ** level_index  10.2 us
    unnamed x54, local copies, waits for them, and re-layouts  10.1 us
    reduce_sum x3, other arithmetic, pool_levels(): pooled = strip_float.reshape(cell_cols // factor, factor, key_rows // fac...  9.77 us
  transfers between devices with their start and end apart: 20, of which 4 were waited for; matrix products, arithmetic and copies ran while one was open for 11% of the time, Pallas kernels for 0%

profile of v1, /device:TPU:1, one launch (start us, length us, event | category | flops | bytes accessed | tf_op | source)
XLA Modules:
  0.0 412.9 jit_solution(15425581410795200754)
XLA Ops:
  7.2 4.6 %reshape.140 = f32[96,2,8,2,256]{4,3,2,1,0:T(2,128)} reshape(bf16[192,16,256]{2,1,0:T(8,128)(2,1)} %param.7) | data formatting | bytes 4718592 | tf_op jit(solution)/shard_map/reshape | solution.py:33
  13.5 2.5 reshape.142
  15.9 2.2 convert_element_type.43
  18.1 4.4 %reduce_sum.27 = f32[96,8,256]{2,1,0:T(8,128)S(1)} reduce(f32[96,2,8,2,256]{4,3,2,1,0:T(2,128)} %reshape.140, f32[]{:T(128)} %constant.6.clone.1), dimensions={1,3}, to_apply=%region_0.0 | reduce | flops 589824 | bytes 3932164 | tf_op jit(solution)/shard_map/reduce_sum | solution.py:35
  22.7 3.0 reduce_sum.32
  25.7 2.4 reduce_sum.33
  28.2 2.8 convolution_bitcast_fusion.2
  31.0 5.2 %fusion.4 = f32[1536,256]{1,0:T(8,128)S(1)} fusion(f32[1536,256]{1,0:T(8,128)S(1)} %convolution_bitcast_fusion.2, bf16[3072,256]{1,0:T(8,128)(2,1)S(1)} %bitcast.277, bf16[1536,4080]{0,1:T(8,128)(2,1)} %bitcast.279), kind=kOutput, calls=%fused_computation.5 | convolution fusion | flops 2416312320 | bytes 14155776 | tf_op jit(solution)/shard_map/dot_general | solution.py:90
  37.8 2.5 fusion.8
  41.1 4.6 %collective-permute-start.12 = (bf16[1,16,256]{2,1,0:T(8,128)(2,1)S(1)}, bf16[1,16,256]{2,1,0:T(8,128)(2,1)S(1)}, u32[]{:S(2)}, u32[]{:S(2)}) collective-permute-start(bf16[1,16,256]{2,1,0:T(8,128)(2,1)S(1)} %get-tuple-element.28), channel_id=1, source_target_pairs={{0,8},{8,16},{16,24},{24,32},{32,40},{40,48},{48,56},{56,64},{64,7... | collective-permute-start | bytes 24584 | tf_op jit(solution)/shard_map/ppermute | solution.py:18
  45.7 2.1 collective-permute-start.13
  52.5 2.9 broadcast_in_dim.6
  55.4 5.2 %div.61 = f32[192,16,256]{2,0,1:T(8,128)} reshape(f32[96,2,8,2,256]{4,1,0,3,2:T(2,128)} %broadcast_in_dim.6) | data formatting | bytes 6291456 | tf_op jit(solution)/shard_map/div | solution.py:101
  61.0 2.3 broadcast_in_dim.7
  63.3 4.9 %div.65 = f32[192,16,256]{2,0,1:T(8,128)} reshape(f32[48,4,4,4,256]{4,1,0,3,2:T(4,128)} %broadcast_in_dim.7) | data formatting | bytes 6291456 | tf_op jit(solution)/shard_map/div | solution.py:101
  68.4 5.4 %fusion = f32[256,3072]{0,1:S(1)} fusion(bf16[1536,256]{1,0:T(8,128)(2,1)S(1)} %bitcast.256, bf16[1536,4080]{0,1:T(8,128)(2,1)} %bitcast.285), kind=kOutput, calls=%fused_computation | convolution fusion | flops 2415919104 | bytes 13369344
  76.7 3.5 copy.54
  81.1 3.6 collective-permute-start.8
  84.7 1.9 collective-permute-start.9
  87.3 3.7 collective-permute-start.14
  93.7 4.6 %collective-permute-start.10 = (bf16[10,1,256]{2,1,0:T(2,128)(2,1)S(1)}, bf16[10,1,256]{2,1,0:T(2,128)(2,1)S(1)}, u32[]{:S(2)}, u32[]{:S(2)}) collective-permute-start(bf16[10,1,256]{2,1,0:T(2,128)(2,1)S(1)} %get-tuple-element.15), channel_id=1, source_target_pairs={{0,1},{1,2},{2,3},{3,4},{4,5},{5,6},{6,7},{8,9},{9,10},{10,11},{11... | collective-permute-start | bytes 15368 | tf_op jit(solution)/shard_map/ppermute | solution.py:18
  99.4 4.5 %collective-permute-start = (bf16[1,24,256]{2,1,0:T(8,128)(2,1)S(1)}, bf16[1,24,256]{2,1,0:T(8,128)(2,1)S(1)}, u32[]{:S(2)}, u32[]{:S(2)}) collective-permute-start(bf16[1,24,256]{2,1,0:T(8,128)(2,1)S(1)} %get-tuple-element.37), channel_id=1, source_target_pairs={{0,8},{8,16},{16,24},{24,32},{32,40},{40,48},{48,56},{56,64},{64,7... | collective-permute-start | bytes 36872 | tf_op jit(solution)/shard_map/ppermute | solution.py:18
  103.9 1.9 collective-permute-start.1
  110.6 4.3 %collective-permute-start.3 = (bf16[10,1,256]{2,1,0:T(2,128)(2,1)S(1)}, bf16[10,1,256]{2,1,0:T(2,128)(2,1)S(1)}, u32[]{:S(2)}, u32[]{:S(2)}) collective-permute-start(bf16[10,1,256]{2,1,0:T(2,128)(2,1)S(1)} %get-tuple-element.20), channel_id=1, source_target_pairs={{0,1},{1,2},{2,3},{3,4},{4,5},{5,6},{6,7},{8,9},{9,10},{10,11},{11... | collective-permute-start | bytes 15368 | tf_op jit(solution)/shard_map/ppermute | solution.py:18
  116.7 44.7 %reduce-scatter.5.cloned.1.call-done = f32[12,16,256]{2,1,0:T(8,128)} async-done(((f32[192,16,256]{2,1,0:T(8,128)}), f32[12,16,256]{2,1,0:T(8,128)}) %reduce-scatter.5.cloned.1.call-update) | async-done | bytes 196624 | tf_op jit(solution)/shard_map/reduce_scatter | solution.py:109
  174.3 4.9 %collective-permute-start.4 = (bf16[1,16,256]{2,1,0:T(8,128)(2,1)S(1)}, bf16[1,16,256]{2,1,0:T(8,128)(2,1)S(1)}, u32[]{:S(2)}, u32[]{:S(2)}) collective-permute-start(bf16[1,16,256]{2,1,0:T(8,128)(2,1)S(1)} %get-tuple-element.33), channel_id=1, source_target_pairs={{0,8},{8,16},{16,24},{24,32},{32,40},{40,48},{48,56},{56,64},{64,7... | collective-permute-start | bytes 24584 | tf_op jit(solution)/shard_map/ppermute | solution.py:18
  179.3 1.9 collective-permute-start.5
  182.1 2.6 collective-permute-done.5
  186.0 4.0 collective-permute-start.7
  190.0 62.1 %all-reduce.3.cloned.1.call-done = f32[3,3,256,256]{3,2,1,0:T(8,128)} async-done(((f32[3,3,256,256]{3,2,1,0:T(8,128)}), f32[3,3,256,256]{3,2,1,0:T(8,128)}) %all-reduce.3.cloned.1.call-update) | async-done | bytes 2359312 | tf_op jit(solution)/shard_map/psum | solution.py:122
  254.8 148.2 %all-reduce.5.cloned.1.call-done = f32[3,3,256,256]{3,2,1,0:T(8,128)} async-done(((f32[3,3,256,256]{3,2,1,0:T(8,128)}), f32[3,3,256,256]{3,2,1,0:T(8,128)}) %all-reduce.5.cloned.1.call-update) | async-done | bytes 2359312 | tf_op jit(solution)/shard_map/psum | solution.py:122
  403.1 3.3 copy.74
  (155 shorter events, 41.6 us)
Async XLA Ops:
  7.2 44.5 %copy-start = (bf16[8,192,256]{2,1,0:T(8,128)(2,1)S(1)}, bf16[8,192,256]{2,1,0:T(8,128)(2,1)}, u32[]{:S(2)}) copy-start(bf16[8,192,256]{2,1,0:T(8,128)(2,1)} %param.6) | copy-start | bytes 2359300
  7.2 4.6 %copy-start.2 = (bf16[192,16,256]{2,1,0:T(8,128)(2,1)S(1)}, bf16[192,16,256]{2,1,0:T(8,128)(2,1)}, u32[]{:S(2)}) copy-start(bf16[192,16,256]{2,1,0:T(8,128)(2,1)} %param.7) | copy-start | bytes 4718596
  7.2 91.2 %reduce-scatter.3.cloned.1.call-start = ((), (), s32[]{:S(2)}) async-start(), calls=%async_computation.2 | async-start | bytes 1769472 | tf_op jit(solution)/shard_map/reduce_scatter | solution.py:102
  28.2 2.8 copy-start.7
  40.3 121.1 %reduce-scatter.5.cloned.1.call-start = ((), (), s32[]{:S(2)}) async-start(), calls=%async_computation.3 | async-start | bytes 3342336 | tf_op jit(solution)/shard_map/reduce_scatter | solution.py:109
  41.1 45.5 %collective-permute-start.12 = (bf16[1,16,256]{2,1,0:T(8,128)(2,1)S(1)}, bf16[1,16,256]{2,1,0:T(8,128)(2,1)S(1)}, u32[]{:S(2)}, u32[]{:S(2)}) collective-permute-start(bf16[1,16,256]{2,1,0:T(8,128)(2,1)S(1)} %get-tuple-element.28), channel_id=1, source_target_pairs={{0,8},{8,16},{16,24},{24,32},{32,40},{40,48},{48,56},{56,64},{64,7... | collective-permute-start | bytes 24584 | tf_op jit(solution)/shard_map/ppermute | solution.py:18
  45.7 41.0 %collective-permute-start.13 = (bf16[1,16,256]{2,1,0:T(8,128)(2,1)S(1)}, bf16[1,16,256]{2,1,0:T(8,128)(2,1)S(1)}, u32[]{:S(2)}, u32[]{:S(2)}) collective-permute-start(bf16[1,16,256]{2,1,0:T(8,128)(2,1)S(1)} %get-tuple-element.27), channel_id=1, source_target_pairs={{8,0},{16,8},{24,16},{32,24},{40,32},{48,40},{56,48},{64,56},{72,6... | collective-permute-start | bytes 24584 | tf_op jit(solution)/shard_map/ppermute | solution.py:20
  68.4 5.7 %copy-start.4 = (f32[192,16,256]{2,0,1:T(8,128)S(1)}, f32[192,16,256]{2,0,1:T(8,128)}, u32[]{:S(2)}) copy-start(f32[192,16,256]{2,0,1:T(8,128)} %div.65) | copy-start | bytes 9437188
  80.2 171.8 %all-reduce.3.cloned.1.call-start = ((), (), s32[]{:S(2)}) async-start(), calls=%async_computation.4 | async-start | bytes 4718592 | tf_op jit(solution)/shard_map/psum | solution.py:122
  81.1 11.3 %collective-permute-start.8 = (bf16[1,24,256]{2,1,0:T(8,128)(2,1)S(1)}, bf16[1,24,256]{2,1,0:T(8,128)(2,1)S(1)}, u32[]{:S(2)}, u32[]{:S(2)}) collective-permute-start(bf16[1,24,256]{2,1,0:T(8,128)(2,1)S(1)} %get-tuple-element.30), channel_id=1, source_target_pairs={{0,8},{8,16},{16,24},{24,32},{32,40},{40,48},{48,56},{56,64},{64,7... | collective-permute-start | bytes 36872 | tf_op jit(solution)/shard_map/ppermute | solution.py:18
  84.7 7.7 %collective-permute-start.9 = (bf16[1,24,256]{2,1,0:T(8,128)(2,1)S(1)}, bf16[1,24,256]{2,1,0:T(8,128)(2,1)S(1)}, u32[]{:S(2)}, u32[]{:S(2)}) collective-permute-start(bf16[1,24,256]{2,1,0:T(8,128)(2,1)S(1)} %get-tuple-element.29), channel_id=1, source_target_pairs={{8,0},{16,8},{24,16},{32,24},{40,32},{48,40},{56,48},{64,56},{72,6... | collective-permute-start | bytes 36872 | tf_op jit(solution)/shard_map/ppermute | solution.py:20
  86.6 19.9 %copy-start.20 = (bf16[1,16,256]{2,1,0:T(8,128)(2,1)}, bf16[1,16,256]{2,1,0:T(8,128)(2,1)S(1)}, u32[]{:S(2)}) copy-start(bf16[1,16,256]{2,1,0:T(8,128)(2,1)S(1)} %collective-permute-done.12) | copy-start | bytes 24580
  86.7 19.9 %copy-start.22 = (bf16[1,16,256]{2,1,0:T(8,128)(2,1)}, bf16[1,16,256]{2,1,0:T(8,128)(2,1)S(1)}, u32[]{:S(2)}) copy-start(bf16[1,16,256]{2,1,0:T(8,128)(2,1)S(1)} %collective-permute-done.13) | copy-start | bytes 24580
  86.7 17.2 %copy-start.18 = (bf16[14,16,256]{2,1,0:T(8,128)(2,1)}, bf16[14,16,256]{2,1,0:T(8,128)(2,1)S(1)}, u32[]{:S(2)}) copy-start(bf16[14,16,256]{2,1,0:T(8,128)(2,1)S(1)} %constant_dynamic-update-slice_fusion.3) | copy-start | bytes 344068
  87.3 76.6 %collective-permute-start.14 = (bf16[14,1,256]{2,1,0:T(2,128)(2,1)S(1)}, bf16[14,1,256]{2,1,0:T(2,128)(2,1)}, u32[]{:S(2)}, u32[]{:S(2)}) collective-permute-start(bf16[14,1,256]{2,1,0:T(2,128)(2,1)S(1)} %get-tuple-element.21), channel_id=1, source_target_pairs={{0,1},{1,2},{2,3},{3,4},{4,5},{5,6},{6,7},{8,9},{9,10},{10,11},{11... | collective-permute-start | bytes 21512 | tf_op jit(solution)/shard_map/ppermute | solution.py:18
  91.1 71.7 %collective-permute-start.15 = (bf16[14,1,256]{2,1,0:T(2,128)(2,1)}, bf16[14,1,256]{2,1,0:T(2,128)(2,1)}, u32[]{:S(2)}, u32[]{:S(2)}) collective-permute-start(bf16[14,1,256]{2,1,0:T(2,128)(2,1)} %get-tuple-element.22), channel_id=1, source_target_pairs={{1,0},{2,1},{3,2},{4,3},{5,4},{6,5},{7,6},{9,8},{10,9},{11,10},{12... | collective-permute-start | bytes 21512 | tf_op jit(solution)/shard_map/ppermute | solution.py:20
  92.4 11.4 %collective-permute-start.11 = (bf16[10,1,256]{2,1,0:T(2,128)(2,1)S(1)}, bf16[10,1,256]{2,1,0:T(2,128)(2,1)S(1)}, u32[]{:S(2)}, u32[]{:S(2)}) collective-permute-start(bf16[10,1,256]{2,1,0:T(2,128)(2,1)S(1)} %get-tuple-element.16), channel_id=1, source_target_pairs={{1,0},{2,1},{3,2},{4,3},{5,4},{6,5},{7,6},{9,8},{10,9},{11,10},{12... | collective-permute-start | bytes 15368 | tf_op jit(solution)/shard_map/ppermute | solution.py:20
  93.7 12.5 %collective-permute-start.10 = (bf16[10,1,256]{2,1,0:T(2,128)(2,1)S(1)}, bf16[10,1,256]{2,1,0:T(2,128)(2,1)S(1)}, u32[]{:S(2)}, u32[]{:S(2)}) collective-permute-start(bf16[10,1,256]{2,1,0:T(2,128)(2,1)S(1)} %get-tuple-element.15), channel_id=1, source_target_pairs={{0,1},{1,2},{2,3},{3,4},{4,5},{5,6},{6,7},{8,9},{9,10},{10,11},{11... | collective-permute-start | bytes 15368 | tf_op jit(solution)/shard_map/ppermute | solution.py:18
  99.4 9.8 %collective-permute-start = (bf16[1,24,256]{2,1,0:T(8,128)(2,1)S(1)}, bf16[1,24,256]{2,1,0:T(8,128)(2,1)S(1)}, u32[]{:S(2)}, u32[]{:S(2)}) collective-permute-start(bf16[1,24,256]{2,1,0:T(8,128)(2,1)S(1)} %get-tuple-element.37), channel_id=1, source_target_pairs={{0,8},{8,16},{16,24},{24,32},{32,40},{40,48},{48,56},{56,64},{64,7... | collective-permute-start | bytes 36872 | tf_op jit(solution)/shard_map/ppermute | solution.py:18
  103.9 5.3 %collective-permute-start.1 = (bf16[1,24,256]{2,1,0:T(8,128)(2,1)S(1)}, bf16[1,24,256]{2,1,0:T(8,128)(2,1)S(1)}, u32[]{:S(2)}, u32[]{:S(2)}) collective-permute-start(bf16[1,24,256]{2,1,0:T(8,128)(2,1)S(1)} %get-tuple-element.38), channel_id=1, source_target_pairs={{8,0},{16,8},{24,16},{32,24},{40,32},{48,40},{56,48},{64,56},{72,6... | collective-permute-start | bytes 36872 | tf_op jit(solution)/shard_map/ppermute | solution.py:20
  108.8 6.7 %copy-start.5 = (bf16[3,3,256,256]{3,2,1,0:T(8,128)(2,1)S(1)}, bf16[3,3,256,256]{3,2,1,0:T(8,128)(2,1)}, u32[]{:S(2)}) copy-start(bf16[3,3,256,256]{3,2,1,0:T(8,128)(2,1)} %param.11) | copy-start | bytes 3538948
  109.1 53.2 %copy-start.10 = (bf16[12,16,256]{2,1,0:T(8,128)(2,1)S(1)}, bf16[12,16,256]{2,1,0:T(8,128)(2,1)}, u32[]{:S(2)}) copy-start(bf16[12,16,256]{2,1,0:T(8,128)(2,1)} %param.10) | copy-start | bytes 294916
  109.2 6.6 %collective-permute-start.2 = (bf16[10,1,256]{2,1,0:T(2,128)(2,1)S(1)}, bf16[10,1,256]{2,1,0:T(2,128)(2,1)S(1)}, u32[]{:S(2)}, u32[]{:S(2)}) collective-permute-start(bf16[10,1,256]{2,1,0:T(2,128)(2,1)S(1)} %get-tuple-element.19), channel_id=1, source_target_pairs={{1,0},{2,1},{3,2},{4,3},{5,4},{6,5},{7,6},{9,8},{10,9},{11,10},{12... | collective-permute-start | bytes 15368 | tf_op jit(solution)/shard_map/ppermute | solution.py:20
  110.6 51.9 %copy-start.23 = (bf16[1,16,256]{2,1,0:T(8,128)(2,1)S(1)}, bf16[1,16,256]{2,1,0:T(8,128)(2,1)}, u32[]{:S(2)}) copy-start(bf16[1,16,256]{2,1,0:T(8,128)(2,1)} %copy-done.22) | copy-start | bytes 24580
  110.6 5.1 %collective-permute-start.3 = (bf16[10,1,256]{2,1,0:T(2,128)(2,1)S(1)}, bf16[10,1,256]{2,1,0:T(2,128)(2,1)S(1)}, u32[]{:S(2)}, u32[]{:S(2)}) collective-permute-start(bf16[10,1,256]{2,1,0:T(2,128)(2,1)S(1)} %get-tuple-element.20), channel_id=1, source_target_pairs={{0,1},{1,2},{2,3},{3,4},{4,5},{5,6},{6,7},{8,9},{9,10},{10,11},{11... | collective-permute-start | bytes 15368 | tf_op jit(solution)/shard_map/ppermute | solution.py:18
  171.9 231.2 %all-reduce.5.cloned.1.call-start = ((), (), s32[]{:S(2)}) async-start(), calls=%async_computation.5 | async-start | bytes 4718592 | tf_op jit(solution)/shard_map/psum | solution.py:122
  173.2 8.0 %copy-start.17 = (bf16[8,24,256]{2,1,0:T(8,128)(2,1)S(1)}, bf16[8,24,256]{2,1,0:T(8,128)(2,1)}, u32[]{:S(2)}) copy-start(bf16[8,24,256]{2,1,0:T(8,128)(2,1)} %get-tuple-element.35) | copy-start | bytes 294916
  174.3 7.7 %collective-permute-start.4 = (bf16[1,16,256]{2,1,0:T(8,128)(2,1)S(1)}, bf16[1,16,256]{2,1,0:T(8,128)(2,1)S(1)}, u32[]{:S(2)}, u32[]{:S(2)}) collective-permute-start(bf16[1,16,256]{2,1,0:T(8,128)(2,1)S(1)} %get-tuple-element.33), channel_id=1, source_target_pairs={{0,8},{8,16},{16,24},{24,32},{32,40},{40,48},{48,56},{56,64},{64,7... | collective-permute-start | bytes 24584 | tf_op jit(solution)/shard_map/ppermute | solution.py:18
  179.3 5.4 %collective-permute-start.5 = (bf16[1,16,256]{2,1,0:T(8,128)(2,1)S(1)}, bf16[1,16,256]{2,1,0:T(8,128)(2,1)S(1)}, u32[]{:S(2)}, u32[]{:S(2)}) collective-permute-start(bf16[1,16,256]{2,1,0:T(8,128)(2,1)S(1)} %get-tuple-element.34), channel_id=1, source_target_pairs={{8,0},{16,8},{24,16},{32,24},{40,32},{48,40},{56,48},{64,56},{72,6... | collective-permute-start | bytes 24584 | tf_op jit(solution)/shard_map/ppermute | solution.py:20
  184.7 67.6 %collective-permute-start.6 = (bf16[14,1,256]{2,1,0:T(2,128)(2,1)S(1)}, bf16[14,1,256]{2,1,0:T(2,128)(2,1)S(1)}, u32[]{:S(2)}, u32[]{:S(2)}) collective-permute-start(bf16[14,1,256]{2,1,0:T(2,128)(2,1)S(1)} %get-tuple-element.25), channel_id=1, source_target_pairs={{1,0},{2,1},{3,2},{4,3},{5,4},{6,5},{7,6},{9,8},{10,9},{11,10},{12... | collective-permute-start | bytes 21512 | tf_op jit(solution)/shard_map/ppermute | solution.py:20
  186.0 66.3 %collective-permute-start.7 = (bf16[14,1,256]{2,1,0:T(2,128)(2,1)S(1)}, bf16[14,1,256]{2,1,0:T(2,128)(2,1)S(1)}, u32[]{:S(2)}, u32[]{:S(2)}) collective-permute-start(bf16[14,1,256]{2,1,0:T(2,128)(2,1)S(1)} %get-tuple-element.26), channel_id=1, source_target_pairs={{0,1},{1,2},{2,3},{3,4},{4,5},{5,6},{6,7},{8,9},{9,10},{10,11},{11... | collective-permute-start | bytes 21512 | tf_op jit(solution)/shard_map/ppermute | solution.py:18
  403.1 3.3 copy-start.1
  (12 other events, 16.4 us)
Sparse Core Ops, SparseCore 0:
  40.4 38.8 reduce-scatter.2
  83.3 77.9 reduce-scatter.4
  172.0 79.9 all-reduce.2
  254.4 148.6 all-reduce.4
